TPU v7x, 256 devices: a whole 4x4x8 slice. The times are simulated.
256 devices in a mesh: past: 32 (over y, x, core), second: 8 (over z).
Axes of the slice: x: 4, y: 4, z: 8, core: 2. Of those that a mesh axis runs over, the one named last changes fastest.
Arguments:
- g_hist: bfloat16 [65536, 8192], P('past', 'second'), may hold values from -6 to 6
- sigma_hist: bfloat16 [1024, 65536], P(None, 'past'), may hold values from -0.046875 to 0.046875
- volterra: bfloat16 [2, 512, 1024], replicated, may hold values from -0.1875 to 0.1875
- sigma_edge: bfloat16 [512, 8192], P(None, 'second'), may hold values from -6 to 6
- coupling: float32 [32, 8192], P(None, 'second'), may hold values from 0.3 to 3
Outputs:
- g_new: bfloat16 [1024, 8192], P(None, 'second')
- sigma_new: bfloat16 [1024, 8192], P(None, 'second')
All inputs are finite; a program needn't handle non-finite values.
Results may differ from a plain program's by a relative error of at most 0.0059.
Values may be sent and summed in bfloat16 or wider, within the bound.
A program may use at most 64 MiB of HBM per device.

v0:
```python
import jax
import jax.numpy as jnp
from jax import lax
from jax.sharding import PartitionSpec as P

N = 32
BLK = 16
NB = 2


def per_device(g_hist, sigma_hist, volterra, sigma_edge, coupling):
    rows = BLK * N
    columns = g_hist.shape[1]
    count_all = rows * columns * lax.axis_size("second")
    prev = sigma_edge
    g_blocks = []
    s_blocks = []
    for block in range(NB):
        sig_rows = sigma_hist[block * rows : (block + 1) * rows, :]
        w_memory = volterra[block][:, :rows]
        w_sigma = volterra[block][:, rows:]
        start_value = jnp.dot(w_sigma, prev, preferred_element_type=jnp.float32)
        mine = lax.psum_scatter(
            jnp.dot(sig_rows, g_hist, preferred_element_type=jnp.float32),
            "past",
            scatter_dimension=0,
            tiled=True,
        ).astype(jnp.bfloat16)
        gnew = start_value + jnp.dot(
            w_memory,
            lax.all_gather(mine, "past", axis=0, tiled=True),
            preferred_element_type=jnp.float32,
        )
        cubic = gnew.reshape(BLK, N, columns) ** 3 * coupling[None]
        local_sq = jnp.sum(cubic * cubic)
        total_sq = lax.psum(local_sq, "second")
        meansq = total_sq / count_all
        sigma = (cubic / jnp.sqrt(meansq + 1e-06)).reshape(rows, columns).astype(jnp.bfloat16)
        g_blocks.append(gnew.astype(jnp.bfloat16))
        s_blocks.append(sigma)
        prev = sigma
    return (jnp.concatenate(g_blocks, axis=0), jnp.concatenate(s_blocks, axis=0))


def solution(mesh):
    return jax.shard_map(
        per_device,
        mesh=mesh,
        in_specs=(P("past", "second"), P(None, "past"), P(), P(None, "second"), P(None, "second")),
        out_specs=(P(None, "second"), P(None, "second")),
        check_vma=False,
    )
```

profile of v0, /device:TPU:2, one launch (start us, length us, event | category | flops | bytes accessed | tf_op | source)
XLA Modules:
  0.0 328.4 jit_solution(678575552743775766)
XLA Ops:
  7.2 0.0 reduce-scatter.3.cloned.1.call-start
  7.2 6.5 %fusion.2 = f32[512,1024]{1,0:T(8,128)} fusion(bf16[2048,1024]{1,0:T(8,128)(2,1)} %param.5, bf16[1024,2048]{1,0:T(8,128)(2,1)} %param.6), kind=kOutput, calls=%fused_computation.14 | convolution fusion | flops 2147483648 | bytes 8388608 | tf_op jit(solution)/shard_map/dot_general | solution.py:24
  13.8 0.0 reduce-scatter.3.cloned.1.call-update
  13.8 0.0 reduce-scatter.5.cloned.1.call-start
  13.8 6.5 %fusion = f32[512,1024]{1,0:T(8,128)} fusion(bf16[2048,1024]{1,0:T(8,128)(2,1)} %param.5, bf16[1024,2048]{1,0:T(8,128)(2,1)} %param.6), kind=kOutput, calls=%fused_computation.10 | convolution fusion | flops 2147483648 | bytes 8388608 | tf_op jit(solution)/shard_map/dot_general | solution.py:24
  20.4 0.0 all-gather.3.cloned.1.call-start
  20.4 82.8 %reduce-scatter.3.cloned.1.call-done = f32[16,1024]{1,0:T(8,128)} async-done(((f32[512,1024]{1,0:T(8,128)}), f32[16,1024]{1,0:T(8,128)}) %reduce-scatter.3.cloned.1.call-update) | async-done | bytes 65552 | tf_op jit(solution)/shard_map/reduce_scatter | solution.py:23
  103.2 1.5 convert_element_type.18
  104.6 0.0 all-gather.3.cloned.1.call-update
  104.7 0.0 all-gather.5.cloned.1.call-start
  104.7 88.8 %reduce-scatter.5.cloned.1.call-done = f32[16,1024]{1,0:T(8,128)} async-done(((f32[512,1024]{1,0:T(8,128)}), f32[16,1024]{1,0:T(8,128)}) %reduce-scatter.5.cloned.1.call-update) | async-done | bytes 65552 | tf_op jit(solution)/shard_map/reduce_scatter | solution.py:23
  193.6 1.4 convert_element_type.21
  195.0 0.0 all-gather.5.cloned.1.call-update
  195.0 1.1 slice_bitcast_fusion
  196.2 1.0 copy-done.4
  197.2 0.7 fusion.8
  197.9 45.8 %all-gather.3.cloned.1.call-done = bf16[512,1024]{1,0:T(8,128)(2,1)} async-done(((bf16[16,1024]{1,0:T(8,128)(2,1)}), bf16[512,1024]{1,0:T(8,128)(2,1)}) %all-gather.3.cloned.1.call-update) | async-done | bytes 1048592 | tf_op jit(solution)/shard_map/all_gather | solution.py:31
  243.7 4.1 %multiply_reduce_fusion.1 = (f32[]{:T(128)}, f32[512,1024]{1,0:T(8,128)}) fusion(f32[32,1024]{1,0:T(8,128)S(1)} %copy-done.7, f32[512,1024]{1,0:T(8,128)S(1)} %fusion.8, bf16[512,1024]{1,0:T(8,128)(2,1)} %all-gather.3.cloned.1.call-done, bf16[512,1024]{1,0:T(8,128)(2,1)} %copy-done.4), kind=kOutput, calls=%fused_computation.13 | convolution fusion | flops 540016640 | bytes 5898244 | tf_op jit(solution)/shard_map/dot_general | solution.py:29
  247.8 18.1 %psum.14 = f32[]{:T(128)} all-reduce(f32[]{:T(128)} %get-tuple-element.6), channel_id=1, replica_groups=mesh['past'=32,'second'=8] {'second'}, use_global_device_ids=true, to_apply=%region_2.0 | all-reduce | flops 1 | bytes 8 | tf_op jit(solution)/shard_map/psum | solution.py:36
  266.6 3.8 %fusion.10 = (bf16[512,1024]{1,0:T(8,128)(2,1)}, bf16[512,1024]{1,0:T(8,128)(2,1)S(1)}) fusion(f32[512,1024]{1,0:T(8,128)} %get-tuple-element.7, f32[]{:T(128)S(6)} %sqrt.6, f32[32,1024]{1,0:T(8,128)S(1)} %copy-done.7), kind=kLoop, calls=%fused_computation.25 | loop fusion | flops 3145728 | bytes 4325380 | tf_op jit(solution)/shard_map/convert_element_type | solution.py:39
  270.4 1.0 copy-done.1
  271.4 2.0 fusion.5
  273.4 19.7 %all-gather.5.cloned.1.call-done = bf16[512,1024]{1,0:T(8,128)(2,1)} async-done(((bf16[16,1024]{1,0:T(8,128)(2,1)}), bf16[512,1024]{1,0:T(8,128)(2,1)}) %all-gather.5.cloned.1.call-update) | async-done | bytes 1048592 | tf_op jit(solution)/shard_map/all_gather | solution.py:31
  293.1 3.8 %bitcast_convert_fusion = (bf16[512,1024]{1,0:T(8,128)(2,1)}, f32[1024,512]{0,1:T(8,128)S(1)}) fusion(f32[1024,512]{0,1:T(8,128)} %fusion.5, bf16[512,1024]{1,0:T(8,128)(2,1)} %all-gather.5.cloned.1.call-done, bf16[512,1024]{1,0:T(8,128)(2,1)} %get-tuple-element.4), kind=kOutput, calls=%fused_computation.6 | convolution fusion | flops 537919488 | bytes 6815744 | tf_op jit(solution)/shard_map/dot_general | solution.py:29
  296.9 1.1 multiply_reduce_fusion
  298.1 18.1 %psum.15 = f32[]{:T(128)} all-reduce(f32[]{:T(128)} %multiply_reduce_fusion), channel_id=1, replica_groups=mesh['past'=32,'second'=8] {'second'}, use_global_device_ids=true, to_apply=%region_5.0 | all-reduce | flops 1 | bytes 8 | tf_op jit(solution)/shard_map/psum | solution.py:36
  316.8 0.3 divide_convert_fusion
  317.2 0.9 copy-done.2
  318.1 1.5 pad_maximum_fusion.1
  319.6 0.0 copy-done.3
  319.6 0.8 copy-done.6
  320.4 1.5 pad_maximum_fusion
  (14 shorter events, 0.0 us)
Async XLA Ops:
  7.2 190.0 %copy-start = (bf16[512,1024]{1,0:T(8,128)(2,1)S(1)}, bf16[512,1024]{1,0:T(8,128)(2,1)}, u32[]{:S(2)}) copy-start(bf16[512,1024]{1,0:T(8,128)(2,1)} %param.8) | copy-start | bytes 3145732
  7.2 96.0 %reduce-scatter.3.cloned.1.call-start = ((), (), s32[]{:S(2)}) async-start(), calls=%async_computation.2 | async-start | bytes 2162688 | tf_op jit(solution)/shard_map/reduce_scatter | solution.py:23
  13.8 179.8 %reduce-scatter.5.cloned.1.call-start = ((), (), s32[]{:S(2)}) async-start(), calls=%async_computation.4 | async-start | bytes 2162688 | tf_op jit(solution)/shard_map/reduce_scatter | solution.py:23
  20.3 174.7 %copy-start.8 = (bf16[2,512,1024]{2,1,0:T(8,128)(2,1)S(1)}, bf16[2,512,1024]{2,1,0:T(8,128)(2,1)}, u32[]{:S(2)}) copy-start(bf16[2,512,1024]{2,1,0:T(8,128)(2,1)} %param.7) | copy-start | bytes 6291460
  20.4 223.4 %all-gather.3.cloned.1.call-start = ((), (), s32[]{:S(2)}) async-start(), calls=%async_computation.3 | async-start | bytes 1081344 | tf_op jit(solution)/shard_map/all_gather | solution.py:31
  104.7 188.5 %all-gather.5.cloned.1.call-start = ((), (), s32[]{:S(2)}) async-start(), calls=%async_computation.5 | async-start | bytes 1081344 | tf_op jit(solution)/shard_map/all_gather | solution.py:31
  196.2 1.0 copy-start.4
  196.2 47.6 %copy-start.7 = (f32[32,1024]{1,0:T(8,128)S(1)}, f32[32,1024]{1,0:T(8,128)}, u32[]{:S(2)}) copy-start(f32[32,1024]{1,0:T(8,128)} %param.9) | copy-start | bytes 393220
  266.6 4.8 %copy-start.5 = (bf16[512,1024]{1,0:T(8,128)(2,1)S(1)}, bf16[512,1024]{1,0:T(8,128)(2,1)}, u32[]{:S(2)}) copy-start(bf16[512,1024]{1,0:T(8,128)(2,1)} %get-tuple-element.4) | copy-start | bytes 3145732
  270.4 1.0 copy-start.1
  316.8 1.2 copy-start.2
  318.1 1.5 copy-start.3
  318.1 2.3 copy-start.6
Sparse Core Ops, SparseCore 0:
  13.9 89.2 reduce-scatter.2
  107.6 85.9 reduce-scatter.4
  196.7 46.9 all-gather.2
  246.1 46.9 all-gather.4
where the time goes:
time: 329 us; the launch traced here: 328 us
  waiting for transfers between devices  237 us (72%)
  blocking collectives  36.2 us (11%)
  matrix products  23.6 us (7%)
  between operations  15.2 us (5%)
  other arithmetic  11.2 us (3%)
  local copies, waits for them, and re-layouts  4.8 us (1%)
    reduce_scatter x2, waiting for transfers between devices, per_device(): lax.psum_scatter(jnp.dot(sig_rows, g_hist, preferred_element_type=jnp.flo...  172 us
    all_gather x2, waiting for transfers between devices, per_device(): lax.all_gather(mine, 'past', axis=0, tiled=True)  65.6 us
    psum x2, blocking collectives, per_device(): total_sq = lax.psum(local_sq, 'second')  36.2 us
    dot_general x2, matrix products, per_device(): jnp.dot(sig_rows, g_hist, preferred_element_type=jnp.float32)  13 us
    dot_general x2, matrix products, per_device(): jnp.dot(w_memory, lax.all_gather(mine, 'past', axis=0, tiled=True), prefe...  7.88 us
  transfers between devices with their start and end apart: 4, of which 4 were waited for; matrix products, arithmetic and copies ran while one was open for 6% of the time, Pallas kernels for 0%

commit v1 on v0

--- a/solution.py
+++ b/solution.py
@@ -6,6 +6,13 @@
 N = 32
 BLK = 16
 NB = 2
+
+
+def gather_over(array, axis, d):
+    size = lax.axis_size(axis)
+    blocks = jnp.stack([array for _ in range(size)])
+    blocks = lax.all_to_all(blocks, axis, split_axis=0, concat_axis=0)
+    return jnp.concatenate(blocks, axis=d)
 
 
 def per_device(g_hist, sigma_hist, volterra, sigma_edge, coupling):
@@ -27,9 +34,7 @@
             tiled=True,
         ).astype(jnp.bfloat16)
         gnew = start_value + jnp.dot(
-            w_memory,
-            lax.all_gather(mine, "past", axis=0, tiled=True),
-            preferred_element_type=jnp.float32,
+            w_memory, gather_over(mine, "past", 0), preferred_element_type=jnp.float32
         )
         cubic = gnew.reshape(BLK, N, columns) ** 3 * coupling[None]
         local_sq = jnp.sum(cubic * cubic)

time: 329 us -> 264 us (0.80)
  waiting for transfers between devices: 237 us -> 165 us
  starting transfers between devices: 0.16 us -> 11.8 us
  other arithmetic: 11.2 us -> 7.52 us
  local copies, waits for them, and re-layouts: 4.8 us -> 8.24 us
    all_gather x2 -> x0, waiting for transfers between devices: 65.6 us -> none  [per_device(): lax.all_gather(mine, 'past', axis=0, tiled=True)]
    all_to_all x0 -> x2, starting transfers between devices: none -> 11.8 us  [gather_over(): blocks = lax.all_to_all(blocks, axis, split_axis=0, concat_axis=0)]
    reduce_scatter x2, waiting for transfers between devices: 172 us -> 165 us  [per_device(): lax.psum_scatter(jnp.dot(sig_rows, g_hist, preferred_element_type=jnp.flo...]
  transfers between devices with their start and end apart: 4 -> 4, of which waited for: 4 -> 2; matrix products, arithmetic and copies ran while one was open for 6% -> 7% of each run, Pallas kernels for 0% -> 0%
where the time goes in v1:
time: 264 us; the launch traced here: 263 us
  waiting for transfers between devices  165 us (62%)
  blocking collectives  33.7 us (13%)
  matrix products  21.1 us (8%)
  between operations  15.5 us (6%)
  starting transfers between devices  11.8 us (4%)
  local copies, waits for them, and re-layouts  8.24 us (3%)
  other arithmetic  7.52 us (3%)
    reduce_scatter x2, waiting for transfers between devices, per_device(): lax.psum_scatter(jnp.dot(sig_rows, g_hist, preferred_element_type=jnp.flo...  165 us
    psum x2, blocking collectives, per_device(): total_sq = lax.psum(local_sq, 'second')  33.7 us
    dot_general x2, matrix products, per_device(): jnp.dot(sig_rows, g_hist, preferred_element_type=jnp.float32)  13 us
    all_to_all x2, starting transfers between devices, gather_over(): blocks = lax.all_to_all(blocks, axis, split_axis=0, concat_axis=0)  11.8 us
    dot_general x2, matrix products, per_device(): jnp.dot(w_memory, gather_over(mine, 'past', 0), preferred_element_type=jn...  5.33 us
  transfers between devices with their start and end apart: 4, of which 2 were waited for; matrix products, arithmetic and copies ran while one was open for 7% of the time, Pallas kernels for 0%

profile of v1, /device:TPU:2, one launch (start us, length us, event | category | flops | bytes accessed | tf_op | source)
XLA Modules:
  0.0 263.4 jit_solution(1361241179617127105)
XLA Ops:
  7.2 0.0 reduce-scatter.3.cloned.1.call-start
  7.2 6.5 %fusion.2 = f32[512,1024]{1,0:T(8,128)} fusion(bf16[2048,1024]{1,0:T(8,128)(2,1)} %param.5, bf16[1024,2048]{1,0:T(8,128)(2,1)} %param.6), kind=kOutput, calls=%fused_computation.14 | convolution fusion | flops 2147483648 | bytes 8388608 | tf_op jit(solution)/shard_map/dot_general | solution.py:31
  13.8 0.0 reduce-scatter.3.cloned.1.call-update
  13.8 0.0 reduce-scatter.5.cloned.1.call-start
  13.8 6.5 %fusion = f32[512,1024]{1,0:T(8,128)} fusion(bf16[2048,1024]{1,0:T(8,128)(2,1)} %param.5, bf16[1024,2048]{1,0:T(8,128)(2,1)} %param.6), kind=kOutput, calls=%fused_computation.10 | convolution fusion | flops 2147483648 | bytes 8388608 | tf_op jit(solution)/shard_map/dot_general | solution.py:31
  20.3 0.0 reduce-scatter.5.cloned.1.call-update
  20.3 82.8 %reduce-scatter.3.cloned.1.call-done = f32[16,1024]{1,0:T(8,128)} async-done(((f32[512,1024]{1,0:T(8,128)}), f32[16,1024]{1,0:T(8,128)}) %reduce-scatter.3.cloned.1.call-update) | async-done | bytes 65552 | tf_op jit(solution)/shard_map/reduce_scatter | solution.py:30
  103.2 0.8 convert_element_type.18
  104.0 1.1 stack.4
  105.1 5.8 %all-to-all-start = ((bf16[32,16,1024]{2,1,0:T(8,128)(2,1)}), bf16[32,16,1024]{2,1,0:T(8,128)(2,1)S(1)}, u32[]{:S(2)}, u32[]{:S(2)}) async-start(bf16[32,16,1024]{2,1,0:T(8,128)(2,1)} %stack.4), calls=%async_computation.1 | async-start | bytes 2097152 | tf_op jit(solution)/shard_map/all_to_all | solution.py:14
  111.0 82.6 %reduce-scatter.5.cloned.1.call-done = f32[16,1024]{1,0:T(8,128)} async-done(((f32[512,1024]{1,0:T(8,128)}), f32[16,1024]{1,0:T(8,128)}) %reduce-scatter.5.cloned.1.call-update) | async-done | bytes 65552 | tf_op jit(solution)/shard_map/reduce_scatter | solution.py:30
  193.6 0.8 convert_element_type.21
  194.4 1.2 stack.5
  195.6 5.9 %all-to-all-start.1 = ((bf16[32,16,1024]{2,1,0:T(8,128)(2,1)}), bf16[32,16,1024]{2,1,0:T(8,128)(2,1)}, u32[]{:S(2)}, u32[]{:S(2)}) async-start(bf16[32,16,1024]{2,1,0:T(8,128)(2,1)} %stack.5), calls=%async_computation.3 | async-start | bytes 2097152 | tf_op jit(solution)/shard_map/all_to_all | solution.py:14
  201.6 2.7 %slice_bitcast_fusion = (bf16[512,1024]{1,0:T(8,128)(2,1)}, bf16[512,1024]{1,0:T(8,128)(2,1)S(1)}) fusion(bf16[2,512,1024]{2,1,0:T(8,128)(2,1)} %param.7), kind=kLoop, calls=%fused_computation.17 | loop fusion | bytes 4194304 | tf_op jit(solution)/shard_map/squeeze | solution.py:28
  204.3 0.7 fusion.8
  205.0 0.2 copy-done.8
  205.2 0.4 copy-done.5
  205.6 1.6 multiply_reduce_fusion.1
  207.1 18.1 %psum.14 = f32[]{:T(128)} all-reduce(f32[]{:T(128)} %get-tuple-element.6), channel_id=1, replica_groups=mesh['past'=32,'second'=8] {'second'}, use_global_device_ids=true, to_apply=%region_2.0 | all-reduce | flops 1 | bytes 8 | tf_op jit(solution)/shard_map/psum | solution.py:41
  225.9 1.4 fusion.10
  227.3 1.0 copy-done.1
  228.2 2.0 fusion.5
  230.3 3.8 %bitcast_convert_fusion = (bf16[512,1024]{1,0:T(8,128)(2,1)}, f32[1024,512]{0,1:T(8,128)S(1)}) fusion(f32[1024,512]{0,1:T(8,128)} %fusion.5, bf16[512,1024]{1,0:T(8,128)(2,1)} %bitcast.5, bf16[512,1024]{1,0:T(8,128)(2,1)} %get-tuple-element.4), kind=kOutput, calls=%fused_computation.6 | convolution fusion | flops 537919488 | bytes 6815744 | tf_op jit(solution)/shard_map/dot_general | solution.py:36
  234.1 1.1 multiply_reduce_fusion
  235.2 15.7 %psum.15 = f32[]{:T(128)} all-reduce(f32[]{:T(128)} %multiply_reduce_fusion), channel_id=1, replica_groups=mesh['past'=32,'second'=8] {'second'}, use_global_device_ids=true, to_apply=%region_5.0 | all-reduce | flops 1 | bytes 8 | tf_op jit(solution)/shard_map/psum | solution.py:41
  251.6 0.3 divide_convert_fusion
  251.9 0.9 copy-done.2
  252.8 1.5 pad_maximum_fusion.1
  254.3 0.0 copy-done.3
  254.3 0.8 copy-done.7
  255.1 1.5 pad_maximum_fusion
  (14 shorter events, 0.0 us)
Async XLA Ops:
  7.2 197.1 %copy-start = (bf16[512,1024]{1,0:T(8,128)(2,1)S(1)}, bf16[512,1024]{1,0:T(8,128)(2,1)}, u32[]{:S(2)}) copy-start(bf16[512,1024]{1,0:T(8,128)(2,1)} %param.8) | copy-start | bytes 3145732
  7.2 96.0 %reduce-scatter.3.cloned.1.call-start = ((), (), s32[]{:S(2)}) async-start(), calls=%async_computation.4 | async-start | bytes 2162688 | tf_op jit(solution)/shard_map/reduce_scatter | solution.py:30
  13.8 179.8 %reduce-scatter.5.cloned.1.call-start = ((), (), s32[]{:S(2)}) async-start(), calls=%async_computation.5 | async-start | bytes 2162688 | tf_op jit(solution)/shard_map/reduce_scatter | solution.py:30
  105.1 89.3 %all-to-all-start = ((bf16[32,16,1024]{2,1,0:T(8,128)(2,1)}), bf16[32,16,1024]{2,1,0:T(8,128)(2,1)S(1)}, u32[]{:S(2)}, u32[]{:S(2)}) async-start(bf16[32,16,1024]{2,1,0:T(8,128)(2,1)} %stack.4), calls=%async_computation.1 | async-start | bytes 2097152 | tf_op jit(solution)/shard_map/all_to_all | solution.py:14
  194.4 9.9 %copy-start.4 = (bf16[32,16,1024]{2,1,0:T(8,128)(2,1)}, bf16[32,16,1024]{2,1,0:T(8,128)(2,1)S(1)}, u32[]{:S(2)}) copy-start(bf16[32,16,1024]{2,1,0:T(8,128)(2,1)S(1)} %all-to-all-done) | copy-start | bytes 3145732
  195.6 34.6 %all-to-all-start.1 = ((bf16[32,16,1024]{2,1,0:T(8,128)(2,1)}), bf16[32,16,1024]{2,1,0:T(8,128)(2,1)}, u32[]{:S(2)}, u32[]{:S(2)}) async-start(bf16[32,16,1024]{2,1,0:T(8,128)(2,1)} %stack.5), calls=%async_computation.3 | async-start | bytes 2097152 | tf_op jit(solution)/shard_map/all_to_all | solution.py:14
  204.3 0.9 copy-start.8
  204.3 1.3 copy-start.5
  225.9 2.4 copy-start.6
  227.3 1.0 copy-start.1
  251.6 1.2 copy-start.2
  252.8 1.5 copy-start.3
  252.8 2.3 copy-start.7
Sparse Core Ops, SparseCore 0:
  13.9 89.2 reduce-scatter.2
  107.6 85.9 reduce-scatter.4
